TPU v7x, 128 devices: a whole 4x4x4 slice. The times are simulated.
128 devices in a mesh: row: 4 (over y), col: 32 (over x, z, core).
Axes of the slice: x: 4, y: 4, z: 4, core: 2. Of those that a mesh axis runs over, the one named last changes fastest.
Arguments:
- charges: float32 [16, 32, 16, 256], P('row', 'col'), may hold values from -6 to 6
- column_order: int32 [32], replicated, may hold values from 0 to 31, as said below
- vertices: float32 [3, 66177], replicated, as said below
- panel_vertices: int32 [3, 131072], replicated, may hold values from 0 to 66176, as said below
- near_pairs: int32 [2, 2048], replicated, may hold values from 0 to 511, as said below
Outputs:
- potential_one: float32 [16, 32, 16, 256], P('row', 'col')
- potential_two: float32 [16, 32, 16, 256], P('row', 'col')
Inputs may be any that keep to these rules, and one draw needn't show every extreme that they name: column_order is a permutation of 0 to 31. `panel_vertices`: panels b * 256 to (b + 1) * 256 - 1 cover block b, a patch of 8 x 16 lattice quads each cut into two triangles along one of its diagonals; vertex ids are lattice row * 513 + lattice column. `vertices`: a jittered lattice of spacing 1.8 in x and y with heights in z; every panel has positive area. `near_pairs`: each column is a pair of distinct block ids, lower first, listed once; the higher block lies at most 3 grid rows below and within squared grid distance 12 of the lower one; entries 512 * b to 512 * (b + 1) - 1 are exactly the pairs whose lower block lies in grid rows 4 * b to 4 * (b + 1) - 1.
All inputs are finite; a program needn't handle non-finite values.
Results may differ from a plain program's by a relative error of at most 0.0003.
Values sent between devices are 32-bit elements; how exact they have to be, the bound alone decides.
A program may use at most 320 MiB of HBM per device.

v0:
```python
import math
import jax
import jax.numpy as jnp
import numpy as np
from jax import lax
from jax.sharding import PartitionSpec as P

PANELS = 256
REACH = 4


def shifted(value, axis, by):
    length = lax.axis_size(axis)
    pairs = [(i, i + by) for i in range(length) if 0 <= i + by < length]
    return lax.ppermute(value, axis, pairs)


def rule_tables():
    gauss_two = np.array([-1.0, 1.0]) / math.sqrt(3.0)
    gauss_four = np.array(
        [-0.8611363115940526, -0.3399810435848563, 0.3399810435848563, 0.8611363115940526]
    )
    weight_four = np.array(
        [0.3478548451374538, 0.6521451548625461, 0.6521451548625461, 0.3478548451374538]
    )
    corner_weights = []
    point_weights = []
    for first_index in range(2):
        for second_index in range(4):
            along = 0.5 * (1.0 + gauss_two[first_index])
            across = 0.5 * (1.0 + gauss_four[second_index])
            corner_weights.append([along, (1.0 - along) * across, (1.0 - along) * (1.0 - across)])
            point_weights.append(2.0 * 0.5 * 0.5 * weight_four[second_index] * (1.0 - along))
    return (np.array(corner_weights), np.array(point_weights))


def block_geometry(vertices, panel_vertices, block_ids):
    panels = panel_vertices.reshape(3, -1, PANELS)[:, block_ids]
    corners = jnp.transpose(vertices[:, panels], (2, 1, 0, 3))
    centre = (corners[:, 0] + corners[:, 1] + corners[:, 2]) / 3.0
    first_edge = corners[:, 1] - corners[:, 0]
    second_edge = corners[:, 2] - corners[:, 0]
    normal_x = first_edge[:, 1] * second_edge[:, 2] - first_edge[:, 2] * second_edge[:, 1]
    normal_y = first_edge[:, 2] * second_edge[:, 0] - first_edge[:, 0] * second_edge[:, 2]
    normal_z = first_edge[:, 0] * second_edge[:, 1] - first_edge[:, 1] * second_edge[:, 0]
    panel_area = 0.5 * jnp.sqrt(normal_x * normal_x + normal_y * normal_y + normal_z * normal_z)
    corner_weights, _ = rule_tables()
    points = jnp.einsum(
        "kc,gcxp->gxkp",
        jnp.asarray(corner_weights, corners.dtype),
        corners,
        precision=lax.Precision.HIGHEST,
    )
    return (centre, points, panel_area)


def tile_block(target, source):
    target_centre, target_points, target_area = target
    source_centre, source_points, source_area = source
    _, point_weights = rule_tables()
    kernel_sum = jnp.zeros(
        (target_centre.shape[0], target_centre.shape[2], source_centre.shape[2]), jnp.float32
    )
    for point_index in range(8):
        weight = float(point_weights[point_index])
        distance = target_centre[:, :, :, None] - source_points[:, :, point_index, None, :]
        kernel_sum = kernel_sum + weight * lax.rsqrt(jnp.sum(distance * distance, axis=1) + 0.01)
        distance = target_points[:, :, point_index, :, None] - source_centre[:, :, None, :]
        kernel_sum = kernel_sum + weight * lax.rsqrt(jnp.sum(distance * distance, axis=1) + 0.01)
    return kernel_sum * target_area[:, :, None] * source_area[:, None, :] / (8.0 * math.pi)


def apply_tiles(source_values, tile_stack):
    return jnp.einsum("grq,gpq->grp", source_values, tile_stack, precision=lax.Precision.HIGHEST)


def apply_transposed(source_values, tile_stack):
    return jnp.einsum("grp,gpq->grq", source_values, tile_stack, precision=lax.Precision.HIGHEST)


def prepare(column_order, vertices, panel_vertices, near_pairs, band_rows):
    columns = lax.axis_size("col")
    band_count = lax.axis_size("row")
    band_index = lax.axis_index("row")
    column_index = lax.axis_index("col")
    positions = jnp.arange(columns, dtype=jnp.int32)
    position_of = jnp.sum(
        jnp.where(column_order[:, None] == positions[None, :], positions[:, None], 0), axis=0
    )
    home_column = jnp.sum(jnp.where(positions == column_index, column_order, 0))
    first_row = band_index * band_rows
    own_blocks = (first_row + jnp.arange(band_rows, dtype=jnp.int32)) * columns + home_column
    band_pairs = near_pairs.shape[1] // band_count
    share = band_pairs // columns
    segment = lax.dynamic_slice_in_dim(
        near_pairs, band_index * band_pairs + column_index * share, share, 1
    )
    low_blocks = segment[0]
    high_blocks = segment[1]
    targets = jnp.concatenate([own_blocks, low_blocks])
    sources = jnp.concatenate([own_blocks, high_blocks])
    tiles = tile_block(
        block_geometry(vertices, panel_vertices, targets),
        block_geometry(vertices, panel_vertices, sources),
    )
    self_tiles = tiles[:band_rows]
    pair_tiles = tiles[band_rows:]
    low_row = low_blocks // columns - first_row
    high_row = high_blocks // columns - first_row
    low_pos = position_of[low_blocks % columns]
    high_pos = position_of[high_blocks % columns]
    slot_table = (low_row, low_pos, high_row, high_pos)
    return (self_tiles, pair_tiles, slot_table)


def near_product(block_values, prepared):
    self_tiles, pair_tiles, slot_table = prepared
    band_rows = block_values.shape[0]
    low_row, low_pos, high_row, high_pos = slot_table
    self_term = apply_tiles(block_values[:, 0], self_tiles)
    later = shifted(block_values[:REACH], "row", -1)
    source_table = lax.all_gather(
        jnp.concatenate([block_values, later], axis=0), "col", axis=1, tiled=True
    )
    to_low = apply_tiles(source_table[high_row, high_pos], pair_tiles)
    to_high = apply_transposed(source_table[low_row, low_pos], pair_tiles)
    partial_value = jnp.zeros(source_table.shape, jnp.float32)
    partial_value = (
        partial_value.at[low_row, low_pos].add(to_low).at[high_row, high_pos].add(to_high)
    )
    summed = lax.psum_scatter(partial_value, "col", scatter_dimension=1, tiled=True)
    carried_down = shifted(summed[band_rows:], "row", 1)
    head = summed[:REACH] + carried_down
    own = jnp.concatenate([head, summed[REACH:band_rows]], axis=0)
    return own + self_term[:, None]


def body(charges, column_order, vertices, panel_vertices, near_pairs):
    prepared = prepare(column_order, vertices, panel_vertices, near_pairs, charges.shape[0])
    potential_one = near_product(charges, prepared)
    potential_two = near_product(potential_one, prepared)
    return (potential_one, potential_two)


def solution(mesh):
    return jax.shard_map(
        body,
        mesh=mesh,
        in_specs=(P("row", "col", None, None), P(), P(), P(), P()),
        out_specs=(P("row", "col", None, None), P("row", "col", None, None)),
        check_vma=False,
    )
```

profile of v0, /device:TPU:8, one launch (start us, length us, event | category | flops | bytes accessed | tf_op | source)
XLA Modules:
  0.0 580.7 jit_solution(6145317578535073538)
XLA Ops:
  7.2 2.4 collective-permute-start
  9.7 0.8 constant_dynamic-slice_fusion
  10.4 1.3 fusion.42
  11.7 0.7 select_reduce_fusion
  12.5 0.7 add_bitcast_fusion
  13.9 16.3 %copy.111 = f32[3,66177]{0,1:T(8,128)} copy(f32[3,66177]{1,0:T(4,128)} %param.9) | data formatting | bytes 1588248 | tf_op args[2]
  30.2 62.1 %gather_fusion.6 = f32[15360,3]{1,0:T(8,128)} fusion(f32[3,66177]{0,1:T(8,128)} %copy.111, s32[15360]{0:T(1024)S(1)} %broadcast_clamp_fusion), kind=kCustom, calls=%fused_computation.6 | custom fusion | bytes 430080 | tf_op jit(solution)/shard_map/gather | solution.py:39
  92.3 5.7 copy.117
  99.6 62.1 %gather_fusion.4 = f32[15360,3]{1,0:T(8,128)} fusion(f32[3,66177]{0,1:T(8,128)} %copy.111, s32[15360]{0:T(1024)S(1)} %broadcast_clamp_fusion.1), kind=kCustom, calls=%fused_computation.4 | custom fusion | bytes 430080 | tf_op jit(solution)/shard_map/gather | solution.py:39
  161.7 5.3 copy.112
  167.1 5.7 copy.120
  173.7 5.3 copy.116
  179.0 0.7 gather_fusion.1
  179.8 0.7 gather_fusion
  181.6 0.6 pad_maximum_fusion
  182.5 34.1 %multiply_reduce_fusion.15 = (f32[20,256,256]{2,1,0:T(8,128)}, f32[20,256,256]{2,1,0:T(8,128)}, f32[20,256,256]{2,1,0:T(8,128)}, f32[20,256,256]{2,1,0:T(8,128)}...) fusion(f32[20,3,256]{2,1,0:T(4,128)S(1)} %copy.119, ...), kind=kLoop, calls=%fused_computation.29 | loop fusion | flops 83886080 | bytes 42496000 | tf_op jit(solution)/shard_map/reduce_sum | solution.py:67
  216.5 33.9 %multiply_reduce_fusion.14 = (f32[20,256,256]{2,1,0:T(8,128)}, f32[20,256,256]{2,1,0:T(8,128)}, f32[20,256,256]{2,1,0:T(8,128)}, f32[20,256,256]{2,1,0:T(8,128)}...) fusion(f32[20,3,256]{2,1,0:T(4,128)S(1)} %copy.123, ...), kind=kLoop, calls=%fused_computation.28 | loop fusion | flops 83886080 | bytes 42496000 | tf_op jit(solution)/shard_map/reduce_sum | solution.py:69
  250.5 29.1 %fusion.15 = f32[20,256,256]{2,1,0:T(8,128)} fusion(f32[20,256,256]{2,1,0:T(8,128)} %get-tuple-element.25, f32[20,256,256]{2,1,0:T(8,128)} %get-tuple-element.17, f32[20,256,256]{2,1,0:T(8,128)} %get-tuple-element.24, f32[20,256,256]{2,1,0:T(8,128)} %get-tuple-element.16, f32[20,256,256]{2,1,0:T(8,128)} %get-tuple-element.23, ...), kind=kLoop, calls=%fused_computation.46 | loop fusion | flops 64225280 | bytes 89169920 | tf_op jit(solution)/shard_map/div | solution.py:70
  279.6 2.8 gather_fusion.2
  282.4 5.7 fusion.22
  288.0 2.8 gather_fusion.7
  290.8 4.3 fusion.20
  295.1 2.6 broadcast.447.clone
  297.7 2.7 scatter_fusion
  300.5 2.6 scatter_fusion.1
  303.0 4.8 copy.152
  307.9 84.7 %reduce-scatter.3.cloned.1.call-done = f32[8,1,16,256]{3,2,0,1:T(8,128)} async-done(((f32[8,32,16,256]{3,2,0,1:T(8,128)}), f32[8,1,16,256]{3,2,0,1:T(8,128)}) %reduce-scatter.3.cloned.1.call-update) | async-done | bytes 131088 | tf_op jit(solution)/shard_map/reduce_scatter | solution.py:131
  392.6 0.8 slice.252
  393.4 3.4 collective-permute-start.1
  396.9 2.7 collective-permute-done.1
  399.6 2.2 fusion.31
  401.8 1.9 collective-permute-start.2
  403.7 4.2 collective-permute-done.2
  408.0 0.7 pad_maximum_fusion.1
  409.0 45.5 %all-gather.5.cloned.1.call-done = f32[8,32,16,256]{3,2,0,1:T(8,128)} async-done(((f32[8,1,16,256]{3,2,0,1:T(8,128)}), f32[8,32,16,256]{3,2,0,1:T(8,128)}) %all-gather.5.cloned.1.call-update) | async-done | bytes 4194320 | tf_op jit(solution)/shard_map/all_gather | solution.py:122
  454.4 2.8 gather_fusion.9
  457.2 4.3 fusion.16
  461.5 2.8 gather_fusion.8
  464.3 5.7 fusion.18
  470.0 2.6 broadcast.447
  472.6 2.7 scatter_fusion.2
  475.3 2.6 scatter_fusion.3
  477.9 4.8 copy.153
  482.8 81.5 %reduce-scatter.5.cloned.1.call-done = f32[8,1,16,256]{3,2,0,1:T(8,128)} async-done(((f32[8,32,16,256]{3,2,0,1:T(8,128)}), f32[8,1,16,256]{3,2,0,1:T(8,128)}) %reduce-scatter.5.cloned.1.call-update) | async-done | bytes 131088 | tf_op jit(solution)/shard_map/reduce_scatter | solution.py:131
  564.3 0.8 slice.254
  565.2 3.4 collective-permute-start.3
  568.6 2.7 collective-permute-done.3
  571.3 2.8 fusion.30
  (84 shorter events, 4.9 us)
Async XLA Ops:
  7.2 6.0 %copy-start = (s32[3,131072]{1,0:T(4,128)S(1)}, s32[3,131072]{1,0:T(4,128)}, u32[]{:S(2)}) copy-start(s32[3,131072]{1,0:T(4,128)} %param.10) | copy-start | bytes 4718596
  7.2 272.4 %all-gather.3.cloned.1.call-start = ((), (), s32[]{:S(2)}) async-start(), calls=%async_computation.2 | async-start | bytes 4325376 | tf_op jit(solution)/shard_map/all_gather | solution.py:122
  7.2 174.3 %collective-permute-start = (f32[4,1,16,256]{3,2,1,0:T(8,128)}, f32[4,1,16,256]{3,2,1,0:T(8,128)S(1)}, u32[]{:S(2)}, u32[]{:S(2)}) collective-permute-start(f32[4,1,16,256]{3,2,1,0:T(8,128)} %param.7), channel_id=1, source_target_pairs={{32,0},{64,32},{96,64},{33,1},{65,33},{97,65},{34,2},{66,34},{98,6... | collective-permute-start | bytes 196616 | tf_op jit(solution)/shard_map/ppermute | solution.py:15
  30.2 67.7 %copy-start.5 = (f32[8,3,1,1]{0,1,3,2:T(4,128)S(1)}, f32[8,3,1,1]{0,1,3,2:T(4,128)}, u32[]{:S(2)}) copy-start(f32[8,3,1,1]{0,1,3,2:T(4,128)} %constant.210) | copy-start | bytes 292
  179.0 2.6 copy-start.4
  182.2 210.4 %reduce-scatter.3.cloned.1.call-start = ((), (), s32[]{:S(2)}) async-start(), calls=%async_computation.3 | async-start | bytes 4325376 | tf_op jit(solution)/shard_map/reduce_scatter | solution.py:131
  216.5 33.9 %copy-start.2 = (f32[20,256,256]{2,1,0:T(8,128)S(1)}, f32[20,256,256]{2,1,0:T(8,128)}, u32[]{:S(2)}) copy-start(f32[20,256,256]{2,1,0:T(8,128)} %get-tuple-element.10) | copy-start | bytes 15728644
  307.9 146.6 %all-gather.5.cloned.1.call-start = ((), (), s32[]{:S(2)}) async-start(), calls=%async_computation.4 | async-start | bytes 4325376 | tf_op jit(solution)/shard_map/all_gather | solution.py:122
  393.4 6.1 %collective-permute-start.1 = (f32[4,1,16,256]{3,2,0,1:T(8,128)S(1)}, f32[4,1,16,256]{3,2,0,1:T(8,128)S(1)}, u32[]{:S(2)}, u32[]{:S(2)}) collective-permute-start(f32[4,1,16,256]{3,2,0,1:T(8,128)S(1)} %slice.252), channel_id=1, source_target_pairs={{0,32},{32,64},{64,96},{1,33},{33,65},{65,97},{2,34},{34,66},{66,9... | collective-permute-start | bytes 196616 | tf_op jit(solution)/shard_map/ppermute | solution.py:15
  401.8 169.5 %copy-start.3 = (f32[4,1,16,256]{3,2,0,1:T(8,128)}, f32[4,1,16,256]{3,2,0,1:T(8,128)S(1)}, u32[]{:S(2)}) copy-start(f32[4,1,16,256]{3,2,0,1:T(8,128)S(1)} %fusion.31) | copy-start | bytes 196612
  401.8 6.2 %collective-permute-start.2 = (f32[4,1,16,256]{3,2,0,1:T(8,128)S(1)}, f32[4,1,16,256]{3,2,0,1:T(8,128)S(1)}, u32[]{:S(2)}, u32[]{:S(2)}) collective-permute-start(f32[4,1,16,256]{3,2,0,1:T(8,128)S(1)} %fusion.31), channel_id=1, source_target_pairs={{32,0},{64,32},{96,64},{33,1},{65,33},{97,65},{34,2},{66,34},{98,6... | collective-permute-start | bytes 196616 | tf_op jit(solution)/shard_map/ppermute | solution.py:15
  408.6 155.7 %reduce-scatter.5.cloned.1.call-start = ((), (), s32[]{:S(2)}) async-start(), calls=%async_computation.5 | async-start | bytes 4325376 | tf_op jit(solution)/shard_map/reduce_scatter | solution.py:131
  475.3 98.8 %copy-start.1 = (s32[3,131072]{1,0:T(4,128)S(1)}, s32[3,131072]{1,0:T(4,128)}, u32[]{:S(2)}) copy-start(s32[3,131072]{1,0:T(4,128)} %param.10) | copy-start | bytes 4718596
  565.2 6.1 %collective-permute-start.3 = (f32[4,1,16,256]{3,2,0,1:T(8,128)S(1)}, f32[4,1,16,256]{3,2,0,1:T(8,128)S(1)}, u32[]{:S(2)}, u32[]{:S(2)}) collective-permute-start(f32[4,1,16,256]{3,2,0,1:T(8,128)S(1)} %slice.254), channel_id=1, source_target_pairs={{0,32},{32,64},{64,96},{1,33},{33,65},{65,97},{2,34},{34,66},{66,9... | collective-permute-start | bytes 196616 | tf_op jit(solution)/shard_map/ppermute | solution.py:15
Sparse Core Ops, SparseCore 0:
  182.3 48.8 all-gather.2
  308.0 84.5 reduce-scatter.2
  408.8 45.6 all-gather.4
  482.9 81.3 reduce-scatter.4
where the time goes:
time: 582 us; the launch traced here: 581 us
  waiting for transfers between devices  221 us (38%)
  local copies, waits for them, and re-layouts  195 us (34%)
  other arithmetic  112 us (19%)
  matrix products  26.2 us (5%)
  between operations  14.4 us (2%)
  starting transfers between devices  11.8 us (2%)
    reduce_scatter x2, waiting for transfers between devices, near_product(): lax.psum_scatter(partial_value, 'col', scatter_dimension=1, tiled=True)  166 us
    gather x4, local copies, waits for them, and re-layouts, block_geometry(): corners = jnp.transpose(vertices[:, panels], (2, 1, 0, 3))  135 us
    reduce_sum x2, other arithmetic, tile_block(): jnp.sum(distance * distance, axis=1) + 0.01  68 us
    all_gather x2, waiting for transfers between devices, near_product(): lax.all_gather(jnp.concatenate([block_values, later], axis=0), 'col', axi...  45.5 us
    div x1, other arithmetic, tile_block(): kernel_sum * target_area[:, :, None] * source_area[:, None, :]  29.1 us
    dot_general x4, matrix products, apply_tiles(): jnp.einsum('grq,gpq->grp', source_values, tile_stack, precision=lax.Preci...  16.4 us
    unnamed x13, local copies, waits for them, and re-layouts  16.3 us
  transfers between devices with their start and end apart: 8, of which 6 were waited for; matrix products, arithmetic and copies ran while one was open for 46% of the time, Pallas kernels for 0%

commit v1 on v0

--- a/solution.py
+++ b/solution.py
@@ -119,8 +119,14 @@
     low_row, low_pos, high_row, high_pos = slot_table
     self_term = apply_tiles(block_values[:, 0], self_tiles)
     later = shifted(block_values[:REACH], "row", -1)
-    source_table = lax.all_gather(
-        jnp.concatenate([block_values, later], axis=0), "col", axis=1, tiled=True
+    source_table = jnp.concatenate(
+        lax.all_to_all(
+            jnp.stack([jnp.concatenate([block_values, later], axis=0)] * lax.axis_size("col")),
+            "col",
+            0,
+            0,
+        ),
+        axis=1,
     )
     to_low = apply_tiles(source_table[high_row, high_pos], pair_tiles)
     to_high = apply_transposed(source_table[low_row, low_pos], pair_tiles)

time: 582 us -> 625 us (1.074)
  blocking collectives: 0 us -> 55.6 us
  waiting for transfers between devices: 221 us -> 195 us
  starting transfers between devices: 11.8 us -> 19.6 us
    all_to_all x0 -> x1, blocking collectives: none -> 55.6 us  [near_product(): lax.all_to_all(jnp.stack([jnp.concatenate([block_values, later], axis=0)]...]
    all_gather x2 -> x0, waiting for transfers between devices: 45.5 us -> none  [near_product(): lax.all_gather(jnp.concatenate([block_values, later], axis=0), 'col', axi...]
    all_to_all x0 -> x1, waiting for transfers between devices: none -> 22.1 us  [near_product(): lax.all_to_all(jnp.stack([jnp.concatenate([block_values, later], axis=0)]...]
    all_to_all x0 -> x1, starting transfers between devices: none -> 8.38 us  [near_product(): lax.all_to_all(jnp.stack([jnp.concatenate([block_values, later], axis=0)]...]
    unnamed x13 -> x11, local copies, waits for them, and re-layouts: 16.3 us -> 16.3 us
  transfers between devices with their start and end apart: 8 -> 7, of which waited for: 6 -> 6; matrix products, arithmetic and copies ran while one was open for 46% -> 44% of each run, Pallas kernels for 0% -> 0%
where the time goes in v1:
time: 625 us; the launch traced here: 623 us
  local copies, waits for them, and re-layouts  198 us (32%)
  waiting for transfers between devices  195 us (31%)
  other arithmetic  114 us (18%)
  blocking collectives  55.6 us (9%)
  matrix products  26.2 us (4%)
  starting transfers between devices  19.6 us (3%)
  between operations  14.6 us (2%)
    reduce_scatter x2, waiting for transfers between devices, near_product(): lax.psum_scatter(partial_value, 'col', scatter_dimension=1, tiled=True)  163 us
    gather x4, local copies, waits for them, and re-layouts, block_geometry(): corners = jnp.transpose(vertices[:, panels], (2, 1, 0, 3))  135 us
    reduce_sum x2, other arithmetic, tile_block(): jnp.sum(distance * distance, axis=1) + 0.01  69.3 us
    all_to_all x1, blocking collectives, near_product(): lax.all_to_all(jnp.stack([jnp.concatenate([block_values, later], axis=0)]...  55.6 us
    div x1, other arithmetic, tile_block(): kernel_sum * target_area[:, :, None] * source_area[:, None, :]  30.6 us
    all_to_all x1, waiting for transfers between devices, near_product(): lax.all_to_all(jnp.stack([jnp.concatenate([block_values, later], axis=0)]...  22.1 us
    dot_general x4, matrix products, apply_tiles(): jnp.einsum('grq,gpq->grp', source_values, tile_stack, precision=lax.Preci...  16.4 us
    unnamed x11, local copies, waits for them, and re-layouts  16.3 us
  transfers between devices with their start and end apart: 7, of which 6 were waited for; matrix products, arithmetic and copies ran while one was open for 44% of the time, Pallas kernels for 0%

profile of v1, /device:TPU:8, one launch (start us, length us, event | category | flops | bytes accessed | tf_op | source)
XLA Modules:
  0.0 623.0 jit_solution(16655237711972097711)
XLA Ops:
  7.2 2.4 collective-permute-start
  9.6 0.8 constant_dynamic-slice_fusion
  10.4 1.3 fusion.42
  11.7 0.7 select_reduce_fusion
  13.9 16.3 %copy.65 = f32[3,66177]{0,1:T(8,128)} copy(f32[3,66177]{1,0:T(4,128)} %param.9) | data formatting | bytes 1588248 | tf_op args[2]
  30.1 62.1 %gather_fusion.6 = f32[15360,3]{1,0:T(8,128)} fusion(f32[3,66177]{0,1:T(8,128)} %copy.65, s32[15360]{0:T(1024)S(1)} %broadcast_clamp_fusion), kind=kCustom, calls=%fused_computation.6 | custom fusion | bytes 430080 | tf_op jit(solution)/shard_map/gather | solution.py:39
  92.2 5.7 copy.71
  100.0 62.1 %gather_fusion.4 = f32[15360,3]{1,0:T(8,128)} fusion(f32[3,66177]{0,1:T(8,128)} %copy.65, s32[15360]{0:T(1024)S(1)} %broadcast_clamp_fusion.1), kind=kCustom, calls=%fused_computation.4 | custom fusion | bytes 430080 | tf_op jit(solution)/shard_map/gather | solution.py:39
  162.1 5.3 copy.66
  167.5 5.7 copy.74
  174.6 5.3 copy.70
  180.0 0.7 gather_fusion.1
  180.7 0.7 gather_fusion
  181.5 35.4 %multiply_reduce_fusion.15 = (f32[20,256,256]{2,1,0:T(8,128)}, f32[20,256,256]{2,1,0:T(8,128)}, f32[20,256,256]{2,1,0:T(8,128)}, f32[20,256,256]{2,1,0:T(8,128)}...) fusion(f32[20,3,256]{2,1,0:T(4,128)S(1)} %copy.73, ...), kind=kLoop, calls=%fused_computation.29 | loop fusion | flops 83886080 | bytes 42496000 | tf_op jit(solution)/shard_map/reduce_sum | solution.py:67
  216.9 33.9 %multiply_reduce_fusion.14 = (f32[20,256,256]{2,1,0:T(8,128)}, f32[20,256,256]{2,1,0:T(8,128)}, f32[20,256,256]{2,1,0:T(8,128)}, f32[20,256,256]{2,1,0:T(8,128)}...) fusion(f32[20,3,256]{2,1,0:T(4,128)S(1)} %copy.77, ...), kind=kLoop, calls=%fused_computation.28 | loop fusion | flops 83886080 | bytes 42496000 | tf_op jit(solution)/shard_map/reduce_sum | solution.py:69
  250.9 2.7 stack.4
  253.5 8.4 %all-to-all-start = ((f32[32,8,1,16,256]{4,3,2,1,0:T(8,128)}), f32[32,8,1,16,256]{4,3,2,1,0:T(8,128)}, u32[]{:S(2)}, u32[]{:S(2)}) async-start(f32[32,8,1,16,256]{4,3,2,1,0:T(8,128)} %stack.4), calls=%async_computation | async-start | bytes 8388608 | tf_op jit(solution)/shard_map/all_to_all | solution.py:123
  261.9 30.6 %fusion.15 = f32[20,256,256]{2,1,0:T(8,128)} fusion(f32[20,256,256]{2,1,0:T(8,128)} %get-tuple-element.23, f32[20,256,256]{2,1,0:T(8,128)} %get-tuple-element.15, f32[20,256,256]{2,1,0:T(8,128)} %get-tuple-element.22, f32[20,256,256]{2,1,0:T(8,128)} %get-tuple-element.14, f32[20,256,256]{2,1,0:T(8,128)} %get-tuple-element.21, ...), kind=kLoop, calls=%fused_computation.46 | loop fusion | flops 64225280 | bytes 89169920 | tf_op jit(solution)/shard_map/div | solution.py:70
  292.5 22.1 %all-to-all-done = f32[32,8,1,16,256]{4,3,2,1,0:T(8,128)} async-done(((f32[32,8,1,16,256]{4,3,2,1,0:T(8,128)}), f32[32,8,1,16,256]{4,3,2,1,0:T(8,128)}, u32[]{:S(2)}, u32[]{:S(2)}) %all-to-all-start) | async-done | bytes 4194336 | tf_op jit(solution)/shard_map/all_to_all | solution.py:123
  314.7 2.8 gather_fusion.7
  317.5 2.8 gather_fusion.2
  320.2 4.3 fusion.20
  324.5 5.7 fusion.22
  330.2 2.6 broadcast.453.clone
  332.8 2.7 scatter_fusion
  335.5 2.6 scatter_fusion.1
  338.1 4.8 copy.106
  343.0 83.0 %reduce-scatter.3.cloned.1.call-done = f32[8,1,16,256]{3,2,0,1:T(8,128)} async-done(((f32[8,32,16,256]{3,2,0,1:T(8,128)}), f32[8,1,16,256]{3,2,0,1:T(8,128)}) %reduce-scatter.3.cloned.1.call-update) | async-done | bytes 131088 | tf_op jit(solution)/shard_map/reduce_scatter | solution.py:137
  426.0 0.8 slice.252
  426.8 3.4 collective-permute-start.1
  430.2 2.7 collective-permute-done.1
  433.0 2.2 fusion.31
  435.2 1.9 collective-permute-start.2
  437.1 4.2 collective-permute-done.2
  441.9 55.6 %all_to_all.10 = f32[32,8,1,16,256]{4,3,2,1,0:T(8,128)} all-to-all(f32[32,8,1,16,256]{4,3,2,1,0:T(8,128)S(1)} %stack.5), channel_id=1, replica_groups=mesh['row'=4,'col'=32] {'col'}, dimensions={0} | all-to-all | bytes 8388608 | tf_op jit(solution)/shard_map/all_to_all | solution.py:123
  497.5 2.8 gather_fusion.9
  500.3 2.8 gather_fusion.8
  503.1 4.3 fusion.16
  507.4 5.7 fusion.18
  513.1 2.6 broadcast.453
  515.7 2.7 scatter_fusion.2
  518.4 2.6 scatter_fusion.3
  521.0 4.8 copy.107
  525.9 80.4 %reduce-scatter.5.cloned.1.call-done = f32[8,1,16,256]{3,2,0,1:T(8,128)} async-done(((f32[8,32,16,256]{3,2,0,1:T(8,128)}), f32[8,1,16,256]{3,2,0,1:T(8,128)}) %reduce-scatter.5.cloned.1.call-update) | async-done | bytes 131088 | tf_op jit(solution)/shard_map/reduce_scatter | solution.py:137
  606.3 0.8 slice.254
  607.2 3.4 collective-permute-start.3
  610.6 2.7 collective-permute-done.3
  613.3 2.8 fusion.30
  (81 shorter events, 5.5 us)
Async XLA Ops:
  7.2 6.0 copy-start
  7.2 243.6 %collective-permute-start = (f32[4,1,16,256]{3,2,1,0:T(8,128)}, f32[4,1,16,256]{3,2,1,0:T(8,128)S(1)}, u32[]{:S(2)}, u32[]{:S(2)}) collective-permute-start(f32[4,1,16,256]{3,2,1,0:T(8,128)} %param.7), channel_id=1, source_target_pairs={{32,0},{64,32},{96,64},{33,1},{65,33},{97,65},{34,2},{66,34},{98,6... | collective-permute-start | bytes 196616 | tf_op jit(solution)/shard_map/ppermute | solution.py:15
  30.1 67.7 %copy-start.4 = (f32[8,3,1,1]{0,1,3,2:T(4,128)S(1)}, f32[8,3,1,1]{0,1,3,2:T(4,128)}, u32[]{:S(2)}) copy-start(f32[8,3,1,1]{0,1,3,2:T(4,128)} %constant.210) | copy-start | bytes 292
  216.9 34.0 %copy-start.3 = (f32[4,1,16,256]{3,2,1,0:T(8,128)S(1)}, f32[4,1,16,256]{3,2,1,0:T(8,128)}, u32[]{:S(2)}) copy-start(f32[4,1,16,256]{3,2,1,0:T(8,128)} %param.7) | copy-start | bytes 196612
  253.5 61.2 %all-to-all-start = ((f32[32,8,1,16,256]{4,3,2,1,0:T(8,128)}), f32[32,8,1,16,256]{4,3,2,1,0:T(8,128)}, u32[]{:S(2)}, u32[]{:S(2)}) async-start(f32[32,8,1,16,256]{4,3,2,1,0:T(8,128)} %stack.4), calls=%async_computation | async-start | bytes 8388608 | tf_op jit(solution)/shard_map/all_to_all | solution.py:123
  261.9 164.1 %reduce-scatter.3.cloned.1.call-start = ((), (), s32[]{:S(2)}) async-start(), calls=%async_computation.4 | async-start | bytes 4325376 | tf_op jit(solution)/shard_map/reduce_scatter | solution.py:137
  343.0 263.4 %reduce-scatter.5.cloned.1.call-start = ((), (), s32[]{:S(2)}) async-start(), calls=%async_computation.5 | async-start | bytes 4325376 | tf_op jit(solution)/shard_map/reduce_scatter | solution.py:137
  426.8 6.1 collective-permute-start.1
  435.2 178.1 %copy-start.2 = (f32[4,1,16,256]{3,2,0,1:T(8,128)}, f32[4,1,16,256]{3,2,0,1:T(8,128)S(1)}, u32[]{:S(2)}) copy-start(f32[4,1,16,256]{3,2,0,1:T(8,128)S(1)} %fusion.31) | copy-start | bytes 196612
  435.2 6.2 collective-permute-start.2
  518.4 97.7 %copy-start.1 = (s32[3,131072]{1,0:T(4,128)S(1)}, s32[3,131072]{1,0:T(4,128)}, u32[]{:S(2)}) copy-start(s32[3,131072]{1,0:T(4,128)} %param.10) | copy-start | bytes 4718596
  607.2 6.1 collective-permute-start.3
Sparse Core Ops, SparseCore 0:
  343.1 82.8 reduce-scatter.2
  526.0 80.2 reduce-scatter.4
